TPU v7x, 32 devices: a whole 2x2x4 slice. The times are simulated.
32 devices in a mesh: row: 8 (over z, core), col: 4 (over y, x).
Axes of the slice: x: 2, y: 2, z: 4, core: 2. Of those that a mesh axis runs over, the one named last changes fastest.
Arguments:
- features: bfloat16 [8192, 256], P(('row', 'col')), may hold values from -6 to 6
- weight_in: bfloat16 [2, 256, 256], replicated, may hold values from -0.21875 to 0.21875
- weight_out: bfloat16 [2, 256, 256], replicated, may hold values from -0.21875 to 0.21875
- weight_self: bfloat16 [2, 256, 256], replicated, may hold values from -0.21875 to 0.21875
- layer_bias: float32 [2, 256], replicated, may hold values from -3 to 3
- out_degree: int32 [8192], P(('row', 'col')), may hold values from 1 to 64
- in_degree: int32 [8192], P(('row', 'col')), may hold values from 1 to 64
- tile_values: bfloat16 [4096, 128, 128], P(('row', 'col')), may hold values from 0 to 1
- tile_pick: int32 [4096], P(('row', 'col')), may hold values from 0 to 3
- tile_count: int32 [32], P(('row', 'col')), may hold values from 1 to 128, as said below
- cotangent: bfloat16 [8192, 256], P(('row', 'col')), may hold values from -6 to 6
Outputs:
- out_features: bfloat16 [8192, 256], P(('row', 'col'))
- grad_features: float32 [8192, 256], P(('row', 'col'))
- grad_weight_in: float32 [2, 256, 256], replicated
- grad_weight_out: float32 [2, 256, 256], replicated
- grad_weight_self: float32 [2, 256, 256], replicated
- grad_bias: float32 [2, 256], replicated
Inputs may be any that keep to these rules, and one draw needn't show every extreme that they name: `tile_count`: slots at or above a device's count are empty and unused; in every draw some device has all 128 slots live. `tile_pick`: slot s of a device belongs to group s // (128 // 32), which fixes the node square of its tile as in the definition of A.
All inputs are finite; a program needn't handle non-finite values.
Results may differ from a plain program's by a relative error of at most 0.025.
Values may be sent and summed in bfloat16 or wider, within the bound.
A program may use at most 128 MiB of HBM per device.

v0:
```python
import jax
import jax.numpy as jnp
from jax import lax
from jax.sharding import PartitionSpec as P


def activation(inputs):
    return jax.nn.gelu(inputs, approximate=True)


def tile_product(
    tile_vals,
    live_mask,
    source_block,
    target_block,
    strip_rows,
    target_blocks,
    transposed_tiles,
    turn_count,
):
    tile_size = tile_vals.shape[1]
    width = strip_rows.shape[1]
    source_blocks = strip_rows.reshape(-1, tile_size, width)
    source_total = source_blocks.shape[0]
    group_size = min(32, tile_vals.shape[0])
    einsum_form = "sji,sjf->sif" if transposed_tiles else "sij,sjf->sif"
    source_ids = jnp.arange(source_total, dtype=jnp.int32)
    target_ids = jnp.arange(target_blocks, dtype=jnp.int32)

    def add_group(turn_index, running):
        first_slot = turn_index * group_size
        tile_part = lax.dynamic_slice_in_dim(tile_vals, first_slot, group_size, 0)
        source_part = lax.dynamic_slice_in_dim(source_block, first_slot, group_size, 0)
        target_part = lax.dynamic_slice_in_dim(target_block, first_slot, group_size, 0)
        active = lax.dynamic_slice_in_dim(live_mask, first_slot, group_size, 0)
        pick_source = (source_part[:, None] == source_ids[None, :]).astype(strip_rows.dtype)
        gathered = jnp.einsum(
            "sb,bjf->sjf", pick_source, source_blocks, preferred_element_type=jnp.float32
        ).astype(strip_rows.dtype)
        product = jnp.einsum(einsum_form, tile_part, gathered, preferred_element_type=jnp.float32)
        place_target = jnp.logical_and(
            target_part[:, None] == target_ids[None, :], active[:, None]
        ).astype(jnp.float32)
        placed = jnp.einsum(
            "st,sif->tif",
            place_target,
            product,
            precision=lax.Precision.HIGHEST,
            preferred_element_type=jnp.float32,
        )
        return running + placed

    start_value = jnp.zeros((target_blocks, tile_size, width), jnp.float32)
    running = lax.fori_loop(0, turn_count, add_group, start_value)
    return running.reshape(target_blocks * tile_size, width)


def per_device(
    features,
    weight_in,
    weight_out,
    weight_self,
    layer_bias,
    out_degree,
    in_degree,
    tile_values,
    tile_pick,
    tile_count,
    cotangent,
):
    row_count = lax.axis_size("row")
    col_count = lax.axis_size("col")
    tile_total = tile_values.shape[0]
    tile_size = tile_values.shape[1]
    own_nodes = features.shape[0]
    sub_blocks = own_nodes // tile_size
    per_peer = tile_total // (row_count * col_count)
    slot_ids = jnp.arange(tile_total, dtype=jnp.int32)
    dest_group = slot_ids // per_peer
    own_rows = dest_group % col_count * sub_blocks + tile_pick // sub_blocks
    own_cols = dest_group // col_count * sub_blocks + tile_pick % sub_blocks
    own_live = slot_ids < tile_count[0]
    group_size = min(32, tile_total)
    own_turns = (tile_count[0] + group_size - 1) // group_size
    row_strip_blocks = col_count * sub_blocks
    col_strip_blocks = row_count * sub_blocks
    scale_in = 1.0 / jnp.sqrt(in_degree.astype(jnp.float32))
    scale_out = 1.0 / jnp.sqrt(out_degree.astype(jnp.float32))

    def forward_messages(first, second):
        column_rows = lax.all_gather(first, "row", axis=0, tiled=True)
        direct = tile_product(
            tile_values,
            own_live,
            own_cols,
            own_rows,
            column_rows,
            row_strip_blocks,
            False,
            own_turns,
        )
        row_rows = lax.all_gather(second, "col", axis=0, tiled=True)
        reverse = tile_product(
            tile_values, own_live, own_rows, own_cols, row_rows, col_strip_blocks, True, own_turns
        )
        summed_direct = lax.psum_scatter(direct, "col", scatter_dimension=0, tiled=True)
        summed_reverse = lax.psum_scatter(reverse, "row", scatter_dimension=0, tiled=True)
        return (summed_direct, summed_reverse)

    layer_total = weight_in.shape[0]
    hidden = features
    stored = []
    for layer in range(layer_total):
        hidden_wide = hidden.astype(jnp.float32)
        scaled_in = (scale_in[:, None] * hidden_wide).astype(jnp.bfloat16)
        scaled_out = (scale_out[:, None] * hidden_wide).astype(jnp.bfloat16)
        summed_direct, summed_reverse = forward_messages(scaled_in, scaled_out)
        msg_in = (scale_out[:, None] * summed_direct).astype(jnp.bfloat16)
        msg_out = (scale_in[:, None] * summed_reverse).astype(jnp.bfloat16)
        preact = jnp.dot(msg_in, weight_in[layer], preferred_element_type=jnp.float32)
        preact = preact + jnp.dot(msg_out, weight_out[layer], preferred_element_type=jnp.float32)
        preact = preact + jnp.dot(hidden, weight_self[layer], preferred_element_type=jnp.float32)
        preact = preact + layer_bias[layer][None, :]
        stored.append((hidden, msg_in, msg_out, preact))
        hidden = activation(preact).astype(jnp.bfloat16)
    out_features = hidden
    upstream = cotangent.astype(jnp.float32)
    grads_in, grads_out, grads_self, grads_bias = ([], [], [], [])
    for layer in reversed(range(layer_total)):
        hidden, msg_in, msg_out, preact = stored[layer]
        unused, pullback = jax.vjp(activation, preact)
        grad_z = pullback(upstream)[0].astype(jnp.bfloat16)
        grads_in.append(jnp.einsum("nf,ng->fg", msg_in, grad_z, preferred_element_type=jnp.float32))
        grads_out.append(
            jnp.einsum("nf,ng->fg", msg_out, grad_z, preferred_element_type=jnp.float32)
        )
        grads_self.append(
            jnp.einsum("nf,ng->fg", hidden, grad_z, preferred_element_type=jnp.float32)
        )
        grads_bias.append(jnp.sum(grad_z.astype(jnp.float32), axis=0))
        back_in = (
            scale_out[:, None]
            * jnp.dot(grad_z, weight_in[layer].T, preferred_element_type=jnp.float32)
        ).astype(jnp.bfloat16)
        back_out = (
            scale_in[:, None]
            * jnp.dot(grad_z, weight_out[layer].T, preferred_element_type=jnp.float32)
        ).astype(jnp.bfloat16)
        backward_summed_direct, backward_summed_reverse = forward_messages(back_out, back_in)
        upstream = (
            scale_out[:, None] * backward_summed_direct
            + scale_in[:, None] * backward_summed_reverse
        )
        upstream = upstream + jnp.dot(
            grad_z, weight_self[layer].T, preferred_element_type=jnp.float32
        )
    local_grads = (
        jnp.stack(grads_in[::-1]),
        jnp.stack(grads_out[::-1]),
        jnp.stack(grads_self[::-1]),
        jnp.stack(grads_bias[::-1]),
    )
    grad_in_all, grad_out_all, grad_self_all, grad_bias_all = lax.psum(
        (local_grads[0], local_grads[1], local_grads[2], local_grads[3]), ("row", "col")
    )
    return (out_features, upstream, grad_in_all, grad_out_all, grad_self_all, grad_bias_all)


def solution(mesh):
    return jax.shard_map(
        per_device,
        mesh=mesh,
        in_specs=(
            P(("row", "col"), None),
            P(),
            P(),
            P(),
            P(),
            P(("row", "col")),
            P(("row", "col")),
            P(("row", "col"), None, None),
            P(("row", "col")),
            P(("row", "col")),
            P(("row", "col"), None),
        ),
        out_specs=(P(("row", "col"), None), P(("row", "col"), None), P(), P(), P(), P()),
        check_vma=False,
    )
```

profile of v0, /device:TPU:0, one launch (start us, length us, event | category | flops | bytes accessed | tf_op | source)
XLA Modules:
  0.0 657.9 jit_solution(3051953045497034110)
XLA Ops:
  10.3 11.5 %all_gather.25 = bf16[1024,256]{1,0:T(8,128)(2,1)S(1)} all-gather(bf16[256,256]{1,0:T(8,128)(2,1)S(1)} %get-tuple-element.740), channel_id=1, replica_groups=mesh['row'=8,'col'=4] {'col'}, dimensions={0}, use_global_device_ids=true | all-gather | bytes 655360 | tf_op jit(solution)/shard_map/all_gather | solution.py:102
  22.5 12.6 %all-gather.5.cloned.1.call-done = bf16[2048,256]{1,0:T(8,128)(2,1)} async-done(((bf16[256,256]{1,0:T(8,128)(2,1)}), bf16[2048,256]{1,0:T(8,128)(2,1)}) %all-gather.5.cloned.1.call-update) | async-done | bytes 1048592 | tf_op jit(solution)/shard_map/all_gather | solution.py:91
  35.2 18.2 %while.88 = (s32[]{:T(128)}, f32[8,128,256]{2,0,1:T(8,128)S(1)}, s32[]{:T(128)}, s32[128]{0:T(128)S(1)}, pred[128]{0:T(512)(128)(4,1)S(1)}, /*index=5*/bf16[128,...) while((s32[]{:T(128)}, f32[8,128,256]{2,0,1:T(8,128)S(1)}, ...), condition=%wide.region_1.2_spmd.clone, body=%wide.region_0.1_spmd.clone.sunk | while | flops 402916352 | bytes 16778268 | solution.py:54
  40.3 4.0 fusion.321
  49.4 4.0 fusion.321
  55.0 17.6 %while.89 = (s32[]{:T(128)}, f32[16,128,256]{2,0,1:T(8,128)S(1)}, s32[]{:T(128)}, s32[128]{0:T(128)S(1)}, pred[128]{0:T(512)(128)(4,1)S(1)}, /*index=5*/bf16[128...) while((s32[]{:T(128)}, f32[16,128,256]{2,0,1:T(8,128)S(1)}, ...), condition=%wide.region_4.5_spmd.clone, body=%wide.region_3.4_spmd.clone.sunk | while | flops 487064832 | bytes 18351132 | solution.py:54
  56.1 3.0 fusion.328
  59.2 4.7 fusion.329
  64.8 2.9 fusion.328
  67.9 4.7 fusion.329
  75.9 23.8 %reduce-scatter.9.cloned.1.call-done = f32[256,256]{1,0:T(8,128)} async-done(((f32[1024,256]{1,0:T(8,128)}), f32[256,256]{1,0:T(8,128)}) %reduce-scatter.9.cloned.1.call-update) | async-done | bytes 262160 | tf_op jit(solution)/shard_map/reduce_scatter | solution.py:106
  100.8 44.9 %reduce-scatter.11.cloned.1.call-done = f32[256,256]{1,0:T(8,128)} async-done(((f32[2048,256]{1,0:T(8,128)}), f32[256,256]{1,0:T(8,128)}) %reduce-scatter.11.cloned.1.call-update) | async-done | bytes 262160 | tf_op jit(solution)/shard_map/reduce_scatter | solution.py:107
  148.7 10.4 %all_gather.27 = bf16[1024,256]{1,0:T(8,128)(2,1)S(1)} all-gather(bf16[256,256]{1,0:T(8,128)(2,1)S(1)} %get-tuple-element.737), channel_id=1, replica_groups=mesh['row'=8,'col'=4] {'col'}, dimensions={0}, use_global_device_ids=true | all-gather | bytes 655360 | tf_op jit(solution)/shard_map/all_gather | solution.py:102
  159.0 10.6 %all-gather.7.cloned.1.call-done = bf16[2048,256]{1,0:T(8,128)(2,1)} async-done(((bf16[256,256]{1,0:T(8,128)(2,1)}), bf16[2048,256]{1,0:T(8,128)(2,1)}) %all-gather.7.cloned.1.call-update) | async-done | bytes 1048592 | tf_op jit(solution)/shard_map/all_gather | solution.py:91
  169.7 18.4 %while.90 = (s32[]{:T(128)}, f32[8,128,256]{2,0,1:T(8,128)S(1)}, s32[]{:T(128)}, s32[128]{0:T(128)S(1)}, pred[128]{0:T(512)(128)(4,1)S(1)}, /*index=5*/bf16[128,...) while((s32[]{:T(128)}, f32[8,128,256]{2,0,1:T(8,128)S(1)}, ...), condition=%wide.region_7.8_spmd.clone, body=%wide.region_6.7_spmd.clone.sunk | while | flops 402916352 | bytes 16778268 | solution.py:54
  175.1 4.0 fusion.337
  184.2 4.0 fusion.337
  190.2 17.8 %while.91 = (s32[]{:T(128)}, f32[16,128,256]{2,0,1:T(8,128)S(1)}, s32[]{:T(128)}, s32[128]{0:T(128)S(1)}, pred[128]{0:T(512)(128)(4,1)S(1)}, /*index=5*/bf16[128...) while((s32[]{:T(128)}, f32[16,128,256]{2,0,1:T(8,128)S(1)}, ...), condition=%wide.region_10.11_spmd.clone, body=%wide.region_9.10_spmd.clone.sunk | while | flops 487064832 | bytes 18351132 | solution.py:54
  194.6 4.7 fusion.345
  200.2 3.0 fusion.344
  203.3 4.7 fusion.345
  210.7 23.7 %reduce-scatter.13.cloned.1.call-done = f32[256,256]{1,0:T(8,128)} async-done(((f32[1024,256]{1,0:T(8,128)}), f32[256,256]{1,0:T(8,128)}) %reduce-scatter.13.cloned.1.call-update) | async-done | bytes 262160 | tf_op jit(solution)/shard_map/reduce_scatter | solution.py:106
  235.6 45.5 %reduce-scatter.15.cloned.1.call-done = f32[256,256]{1,0:T(8,128)} async-done(((f32[2048,256]{1,0:T(8,128)}), f32[256,256]{1,0:T(8,128)}) %reduce-scatter.15.cloned.1.call-update) | async-done | bytes 262160 | tf_op jit(solution)/shard_map/reduce_scatter | solution.py:107
  284.7 10.2 %all_gather.29 = bf16[1024,256]{1,0:T(8,128)(2,1)S(1)} all-gather(bf16[256,256]{1,0:T(8,128)(2,1)S(1)} %fusion.179), channel_id=1, replica_groups=mesh['row'=8,'col'=4] {'col'}, dimensions={0}, use_global_device_ids=true | all-gather | bytes 655360 | tf_op jit(solution)/shard_map/all_gather | solution.py:102
  294.8 10.4 %all-gather.9.cloned.1.call-done = bf16[2048,256]{1,0:T(8,128)(2,1)} async-done(((bf16[256,256]{1,0:T(8,128)(2,1)}), bf16[2048,256]{1,0:T(8,128)(2,1)}) %all-gather.9.cloned.1.call-update) | async-done | bytes 1048592 | tf_op jit(solution)/shard_map/all_gather | solution.py:91
  305.3 18.3 %while.92 = (s32[]{:T(128)}, f32[8,128,256]{2,0,1:T(8,128)S(1)}, s32[]{:T(128)}, s32[128]{0:T(128)S(1)}, pred[128]{0:T(512)(128)(4,1)S(1)}, /*index=5*/bf16[128,...) while((s32[]{:T(128)}, f32[8,128,256]{2,0,1:T(8,128)S(1)}, ...), condition=%wide.region_13.14_spmd.clone, body=%wide.region_12.13_spmd.clone.sunk | while | flops 402916352 | bytes 16778268 | solution.py:54
  310.6 4.0 fusion.353
  319.7 4.0 fusion.353
  325.8 17.6 %while.93 = (s32[]{:T(128)}, f32[16,128,256]{2,0,1:T(8,128)S(1)}, s32[]{:T(128)}, s32[128]{0:T(128)S(1)}, pred[128]{0:T(512)(128)(4,1)S(1)}, /*index=5*/bf16[128...) while((s32[]{:T(128)}, f32[16,128,256]{2,0,1:T(8,128)S(1)}, ...), condition=%wide.region_16.17_spmd.clone, body=%wide.region_15.16_spmd.clone.sunk | while | flops 487064832 | bytes 18351132 | solution.py:54
  329.9 4.7 fusion.361
  335.5 3.0 fusion.360
  338.6 4.7 fusion.361
  346.0 23.9 %reduce-scatter.17.cloned.1.call-done = f32[256,256]{1,0:T(8,128)} async-done(((f32[1024,256]{1,0:T(8,128)}), f32[256,256]{1,0:T(8,128)}) %reduce-scatter.17.cloned.1.call-update) | async-done | bytes 262160 | tf_op jit(solution)/shard_map/reduce_scatter | solution.py:106
  370.0 46.4 %reduce-scatter.19.cloned.1.call-done = f32[256,256]{1,0:T(8,128)} async-done(((f32[2048,256]{1,0:T(8,128)}), f32[256,256]{1,0:T(8,128)}) %reduce-scatter.19.cloned.1.call-update) | async-done | bytes 262160 | tf_op jit(solution)/shard_map/reduce_scatter | solution.py:107
  419.8 10.3 %all_gather.31 = bf16[1024,256]{1,0:T(8,128)(2,1)S(1)} all-gather(bf16[256,256]{1,0:T(8,128)(2,1)S(1)} %fusion.181), channel_id=1, replica_groups=mesh['row'=8,'col'=4] {'col'}, dimensions={0}, use_global_device_ids=true | all-gather | bytes 655360 | tf_op jit(solution)/shard_map/all_gather | solution.py:102
  433.6 6.1 all-gather.11.cloned.1.call-done
  439.7 18.4 %while.94 = (s32[]{:T(128)}, f32[8,128,256]{2,0,1:T(8,128)S(1)}, s32[]{:T(128)}, s32[128]{0:T(128)S(1)}, pred[128]{0:T(512)(128)(4,1)S(1)}, /*index=5*/bf16[128,...) while((s32[]{:T(128)}, f32[8,128,256]{2,0,1:T(8,128)S(1)}, ...), condition=%wide.region_19.20_spmd.clone, body=%wide.region_18.19_spmd.clone.sunk | while | flops 402916352 | bytes 16778268 | solution.py:54
  445.1 4.0 fusion.369
  454.2 4.0 fusion.369
  459.8 17.7 %while.95 = (s32[]{:T(128)}, f32[16,128,256]{2,0,1:T(8,128)S(1)}, s32[]{:T(128)}, s32[128]{0:T(128)S(1)}, pred[128]{0:T(512)(128)(4,1)S(1)}, /*index=5*/bf16[128...) while((s32[]{:T(128)}, f32[16,128,256]{2,0,1:T(8,128)S(1)}, ...), condition=%wide.region_22.23_spmd.clone, body=%wide.region_21.22_spmd.clone.sunk | while | flops 487064832 | bytes 18351132 | solution.py:54
  460.9 3.0 fusion.376
  464.1 4.7 fusion.377
  469.6 3.0 fusion.376
  472.8 4.7 fusion.377
  480.1 74.3 %psum.31 = f32[2,256]{1,0:T(2,128)} all-reduce(f32[2,256]{1,0:T(2,128)S(1)} %pad_maximum_fusion.3), channel_id=1, replica_groups=mesh['row'=8,'col'=4] {'row','col'}, use_global_device_ids=true, to_apply=%region_29.30 | all-reduce | flops 512 | bytes 4096 | tf_op jit(solution)/shard_map/psum | solution.py:163
  554.4 24.9 %all-reduce.3.cloned.1.call-done = (f32[2,256,256]{2,1,0:T(8,128)}, f32[2,256,256]{2,1,0:T(8,128)}, f32[2,256,256]{1,2,0:T(8,128)}) async-done(((f32[2,256,256]{2,1,0:T(8,128)}, f32[2,256,256]{2,1,0:T(8,128)}, f32[2,256,256]{1,2,0:T(8,128)}), (f32[2,256,256]{2,1,0:T(8,128)}, f32[2,256,256]{2,1,0:T(8,128)}, f32[2,256,256]{1,2,0:T(8,128)})) %all-reduce.3.cloned.1.call-update) | async-done | bytes 1572880 | tf_op jit(solution)/shard_map/psum | solution.py:163
  581.4 27.6 %reduce-scatter.21.cloned.1.call-done = f32[256,256]{1,0:T(8,128)} async-done(((f32[1024,256]{1,0:T(8,128)}), f32[256,256]{1,0:T(8,128)}) %reduce-scatter.21.cloned.1.call-update) | async-done | bytes 262160 | tf_op jit(solution)/shard_map/reduce_scatter | solution.py:106
  609.0 38.3 %reduce-scatter.23.cloned.1.call-done = f32[256,256]{1,0:T(8,128)} async-done(((f32[2048,256]{1,0:T(8,128)}), f32[256,256]{1,0:T(8,128)}) %reduce-scatter.23.cloned.1.call-update) | async-done | bytes 262160 | tf_op jit(solution)/shard_map/reduce_scatter | solution.py:107
  (215 shorter events, 97.1 us)
Async XLA Ops:
  7.2 28.0 %all-gather.5.cloned.1.call-start = ((), (), s32[]{:S(2)}) async-start(), calls=%async_computation.8 | async-start | bytes 1179648 | tf_op jit(solution)/shard_map/all_gather | solution.py:91
  9.6 90.0 %reduce-scatter.9.cloned.1.call-start = ((), (), s32[]{:S(2)}) async-start(), calls=%async_computation.9 | async-start | bytes 1310720 | tf_op jit(solution)/shard_map/reduce_scatter | solution.py:106
  54.7 91.0 %reduce-scatter.11.cloned.1.call-start = ((), (), s32[]{:S(2)}) async-start(), calls=%async_computation.10 | async-start | bytes 2359296 | tf_op jit(solution)/shard_map/reduce_scatter | solution.py:107
  75.2 0.7 copy-start.14
  75.2 24.5 %copy-start = (bf16[2,256,256]{2,1,0:T(8,128)(2,1)S(1)}, bf16[2,256,256]{2,1,0:T(8,128)(2,1)}, u32[]{:S(2)}) copy-start(bf16[2,256,256]{2,1,0:T(8,128)(2,1)} %param.28) | copy-start | bytes 786436
  75.2 70.5 %copy-start.3 = (bf16[2,256,256]{2,1,0:T(8,128)(2,1)S(1)}, bf16[2,256,256]{2,1,0:T(8,128)(2,1)}, u32[]{:S(2)}) copy-start(bf16[2,256,256]{2,1,0:T(8,128)(2,1)} %param.29) | copy-start | bytes 786436
  75.2 71.7 %copy-start.8 = (bf16[256,256]{1,0:T(8,128)(2,1)S(1)}, bf16[256,256]{1,0:T(8,128)(2,1)}, u32[]{:S(2)}) copy-start(bf16[256,256]{1,0:T(8,128)(2,1)} %param.27) | copy-start | bytes 393220
  75.2 71.7 %copy-start.11 = (bf16[2,256,256]{2,1,0:T(8,128)(2,1)S(1)}, bf16[2,256,256]{2,1,0:T(8,128)(2,1)}, u32[]{:S(2)}) copy-start(bf16[2,256,256]{2,1,0:T(8,128)(2,1)} %param.30) | copy-start | bytes 786436
  75.2 94.4 %all-gather.7.cloned.1.call-start = ((), (), s32[]{:S(2)}) async-start(), calls=%async_computation.11 | async-start | bytes 1179648 | tf_op jit(solution)/shard_map/all_gather | solution.py:91
  147.8 134.5 %copy-start.9 = (bf16[256,256]{1,0:T(8,128)(2,1)}, bf16[256,256]{1,0:T(8,128)(2,1)S(1)}, u32[]{:S(2)}) copy-start(bf16[256,256]{1,0:T(8,128)(2,1)S(1)} %get-tuple-element.738) | copy-start | bytes 393220
  148.6 85.8 %reduce-scatter.13.cloned.1.call-start = ((), (), s32[]{:S(2)}) async-start(), calls=%async_computation.12 | async-start | bytes 1310720 | tf_op jit(solution)/shard_map/reduce_scatter | solution.py:106
  188.1 1.4 copy-start.16
  188.2 1.4 copy-start.21
  188.2 1.4 copy-start.27
  189.5 91.7 %reduce-scatter.15.cloned.1.call-start = ((), (), s32[]{:S(2)}) async-start(), calls=%async_computation.13 | async-start | bytes 2359296 | tf_op jit(solution)/shard_map/reduce_scatter | solution.py:107
  189.6 0.7 copy-start.17
  189.6 0.7 copy-start.22
  189.6 0.7 copy-start.28
  210.6 71.7 %copy-start.12 = (bf16[2,256,256]{2,1,0:T(8,128)(2,1)S(1)}, bf16[2,256,256]{2,1,0:T(8,128)(2,1)}, u32[]{:S(2)}) copy-start(bf16[2,256,256]{2,1,0:T(8,128)(2,1)} %param.30) | copy-start | bytes 786436
  210.7 71.7 %copy-start.15 = (bf16[256,256]{1,0:T(8,128)(2,1)S(1)}, bf16[256,256]{1,0:T(8,128)(2,1)}, u32[]{:S(2)}) copy-start(bf16[256,256]{1,0:T(8,128)(2,1)} %param.37) | copy-start | bytes 393220
  210.7 94.6 %all-gather.9.cloned.1.call-start = ((), (), s32[]{:S(2)}) async-start(), calls=%async_computation.14 | async-start | bytes 1179648 | tf_op jit(solution)/shard_map/all_gather | solution.py:91
  282.4 22.9 %copy-start.18 = (pred[128]{0:T(512)(128)(4,1)S(1)}, pred[128]{0:T(512)(128)(4,1)}, u32[]{:S(2)}) copy-start(pred[128]{0:T(512)(128)(4,1)} %copy-done.16) | copy-start | bytes 388
  282.4 22.9 %copy-start.23 = (s32[128]{0:T(128)S(1)}, s32[128]{0:T(128)}, u32[]{:S(2)}) copy-start(s32[128]{0:T(128)} %copy-done.21) | copy-start | bytes 1540
  282.4 22.9 %copy-start.29 = (s32[128]{0:T(128)S(1)}, s32[128]{0:T(128)}, u32[]{:S(2)}) copy-start(s32[128]{0:T(128)} %copy-done.27) | copy-start | bytes 1540
  284.4 85.6 %reduce-scatter.17.cloned.1.call-start = ((), (), s32[]{:S(2)}) async-start(), calls=%async_computation.15 | async-start | bytes 1310720 | tf_op jit(solution)/shard_map/reduce_scatter | solution.py:106
  323.7 1.4 copy-start.19
  323.7 1.4 copy-start.24
  323.7 1.4 copy-start.30
  325.0 91.3 %reduce-scatter.19.cloned.1.call-start = ((), (), s32[]{:S(2)}) async-start(), calls=%async_computation.16 | async-start | bytes 2359296 | tf_op jit(solution)/shard_map/reduce_scatter | solution.py:107
  325.1 0.7 copy-start.20
  325.1 0.7 copy-start.25
  325.1 0.7 copy-start.31
  345.9 70.4 %copy-start.13 = (bf16[2,256,256]{2,1,0:T(8,128)(2,1)S(1)}, bf16[2,256,256]{2,1,0:T(8,128)(2,1)}, u32[]{:S(2)}) copy-start(bf16[2,256,256]{2,1,0:T(8,128)(2,1)} %param.30) | copy-start | bytes 786436
  345.9 70.4 %copy-start.33 = (f32[256,256]{1,0:T(8,128)S(1)}, f32[256,256]{1,0:T(8,128)}, u32[]{:S(2)}) copy-start(f32[256,256]{1,0:T(8,128)} %get-tuple-element.746) | copy-start | bytes 786436
  345.9 72.8 %copy-start.10 = (bf16[256,256]{1,0:T(8,128)(2,1)S(1)}, bf16[256,256]{1,0:T(8,128)(2,1)}, u32[]{:S(2)}) copy-start(bf16[256,256]{1,0:T(8,128)(2,1)} %copy-done.9) | copy-start | bytes 393220
  345.9 73.0 %copy-start.2 = (f32[256,256]{1,0:T(8,128)S(1)}, f32[256,256]{1,0:T(8,128)}, u32[]{:S(2)}) copy-start(f32[256,256]{1,0:T(8,128)} %reduce-scatter.13.cloned.1.call-done) | copy-start | bytes 786436
  346.0 73.3 %copy-start.5 = (f32[256,256]{1,0:T(8,128)S(1)}, f32[256,256]{1,0:T(8,128)}, u32[]{:S(2)}) copy-start(f32[256,256]{1,0:T(8,128)} %reduce-scatter.15.cloned.1.call-done) | copy-start | bytes 786436
  346.0 93.7 %all-gather.11.cloned.1.call-start = ((), (), s32[]{:S(2)}) async-start(), calls=%async_computation.17 | async-start | bytes 1179648 | tf_op jit(solution)/shard_map/all_gather | solution.py:91
  417.8 12.4 %copy-start.1 = (f32[256,256]{1,0:T(8,128)S(1)}, f32[256,256]{1,0:T(8,128)}, u32[]{:S(2)}) copy-start(f32[256,256]{1,0:T(8,128)} %reduce-scatter.9.cloned.1.call-done) | copy-start | bytes 786436
  418.7 160.6 %all-reduce.3.cloned.1.call-start = ((), (), s32[]{:S(2)}) async-start(), calls=%async_computation.20 | async-start | bytes 3145728 | tf_op jit(solution)/shard_map/psum | solution.py:163
  419.0 12.3 %copy-start.4 = (f32[256,256]{1,0:T(8,128)S(1)}, f32[256,256]{1,0:T(8,128)}, u32[]{:S(2)}) copy-start(f32[256,256]{1,0:T(8,128)} %reduce-scatter.11.cloned.1.call-done) | copy-start | bytes 786436
  432.4 7.3 %copy-start.26 = (s32[128]{0:T(128)S(1)}, s32[128]{0:T(128)}, u32[]{:S(2)}) copy-start(s32[128]{0:T(128)} %copy-done.24) | copy-start | bytes 1540
  432.4 7.3 %copy-start.32 = (s32[128]{0:T(128)S(1)}, s32[128]{0:T(128)}, u32[]{:S(2)}) copy-start(s32[128]{0:T(128)} %copy-done.30) | copy-start | bytes 1540
  433.5 175.5 %reduce-scatter.21.cloned.1.call-start = ((), (), s32[]{:S(2)}) async-start(), calls=%async_computation.18 | async-start | bytes 1310720 | tf_op jit(solution)/shard_map/reduce_scatter | solution.py:106
  459.5 187.8 %reduce-scatter.23.cloned.1.call-start = ((), (), s32[]{:S(2)}) async-start(), calls=%async_computation.19 | async-start | bytes 2359296 | tf_op jit(solution)/shard_map/reduce_scatter | solution.py:107
  579.3 70.0 %copy-start.7 = (f32[2,256,256]{2,1,0:T(8,128)S(1)}, f32[2,256,256]{2,1,0:T(8,128)}, u32[]{:S(2)}) copy-start(f32[2,256,256]{2,1,0:T(8,128)} %get-tuple-element.1441) | copy-start | bytes 1572868
  579.3 70.8 %copy-start.6 = (f32[2,256,256]{2,1,0:T(8,128)S(1)}, f32[2,256,256]{2,1,0:T(8,128)}, u32[]{:S(2)}) copy-start(f32[2,256,256]{2,1,0:T(8,128)} %get-tuple-element.1442) | copy-start | bytes 1572868
Sparse Core Ops, SparseCore 0:
  10.1 24.9 all-gather.4
  54.8 44.7 reduce-scatter.8
  101.9 43.6 reduce-scatter.10
  148.7 20.8 all-gather.6
  189.6 44.8 reduce-scatter.12
  236.6 44.5 reduce-scatter.14
  284.5 20.6 all-gather.8
  325.1 44.7 reduce-scatter.16
  372.3 44.0 reduce-scatter.18
  418.8 20.7 all-gather.10
  445.8 133.3 all-reduce.2
  582.0 26.9 reduce-scatter.20
  611.3 35.9 reduce-scatter.22
where the time goes:
time: 665 us; the launch traced here: 658 us
  waiting for transfers between devices  339 us (51%)
  matrix products  152 us (23%)
  blocking collectives  117 us (18%)
  local copies, waits for them, and re-layouts  25.6 us (4%)
  between operations  15.6 us (2%)
    reduce_scatter x4, waiting for transfers between devices, forward_messages(): lax.psum_scatter(reverse, 'row', scatter_dimension=0, tiled=True)  175 us
    reduce_scatter x4, waiting for transfers between devices, forward_messages(): lax.psum_scatter(direct, 'col', scatter_dimension=0, tiled=True)  99.1 us
    psum x1, blocking collectives, per_device(): lax.psum((local_grads[0], local_grads[1], local_grads[2], local_grads[3])...  74.3 us
    dot_general x16, matrix products, add_group(): jnp.einsum('st,sif->tif', place_target, product, precision=lax.Precision....  69.7 us
    dot_general x16, matrix products, add_group(): jnp.einsum(einsum_form, tile_part, gathered, preferred_element_type=jnp.f...  45.8 us
    all_gather x4, blocking collectives, forward_messages(): row_rows = lax.all_gather(second, 'col', axis=0, tiled=True)  42.4 us
    all_gather x4, waiting for transfers between devices, forward_messages(): column_rows = lax.all_gather(first, 'row', axis=0, tiled=True)  39.7 us
    psum x1, waiting for transfers between devices, per_device(): lax.psum((local_grads[0], local_grads[1], local_grads[2], local_grads[3])...  24.9 us
  transfers between devices with their start and end apart: 13, of which 13 were waited for; matrix products, arithmetic and copies ran while one was open for 17% of the time, Pallas kernels for 0%

commit v1 on v0

v1 whole, which is shorter than its diff:
```python
import jax
import jax.numpy as jnp
from jax import lax
from jax.sharding import PartitionSpec as P


def activation(inputs):
    return jax.nn.gelu(inputs, approximate=True)


def dense_block(tile_values, tile_pick, tile_count, row_count, col_count, sub_blocks):
    tile_total, tile_size, unused = tile_values.shape
    per_peer = tile_total // (row_count * col_count)
    live = jnp.arange(tile_total, dtype=jnp.int32) < tile_count[0]
    picks = jnp.where(live, tile_pick, -1).reshape(row_count * col_count, per_peer)
    tiles = tile_values.reshape(row_count * col_count, per_peer, tile_size, tile_size)
    rows = []
    for row_half in range(sub_blocks):
        cols = []
        for col_half in range(sub_blocks):
            spot = row_half * sub_blocks + col_half
            total = 0.0
            for slot in range(per_peer):
                total = total + jnp.where(
                    (picks[:, slot] == spot)[:, None, None], tiles[:, slot].astype(jnp.float32), 0.0
                )
            cols.append(total.astype(jnp.bfloat16))
        rows.append(jnp.concatenate(cols, axis=2))
    squares = jnp.concatenate(rows, axis=1)
    side = sub_blocks * tile_size
    squares = squares.reshape(row_count, col_count, side, side)
    return squares.transpose(1, 2, 0, 3).reshape(col_count * side, row_count * side)


def per_device(
    features,
    weight_in,
    weight_out,
    weight_self,
    layer_bias,
    out_degree,
    in_degree,
    tile_values,
    tile_pick,
    tile_count,
    cotangent,
):
    row_count = lax.axis_size("row")
    col_count = lax.axis_size("col")
    sub_blocks = features.shape[0] // tile_values.shape[1]
    block = dense_block(tile_values, tile_pick, tile_count, row_count, col_count, sub_blocks)
    scale_in = 1.0 / jnp.sqrt(in_degree.astype(jnp.float32))
    scale_out = 1.0 / jnp.sqrt(out_degree.astype(jnp.float32))

    def forward_messages(first, second):
        row_rows = lax.all_gather(second, "col", axis=0, tiled=True)
        column_rows = lax.all_gather(first, "row", axis=0, tiled=True)
        reverse = lax.dot_general(
            block, row_rows, (((0,), (0,)), ((), ())), preferred_element_type=jnp.float32
        )
        direct = jnp.dot(block, column_rows, preferred_element_type=jnp.float32)
        summed_reverse = lax.psum_scatter(reverse, "row", scatter_dimension=0, tiled=True)
        summed_direct = lax.psum_scatter(direct, "col", scatter_dimension=0, tiled=True)
        return (summed_direct, summed_reverse)

    layer_total = weight_in.shape[0]
    hidden = features
    stored = []
    for layer in range(layer_total):
        hidden_wide = hidden.astype(jnp.float32)
        scaled_in = (scale_in[:, None] * hidden_wide).astype(jnp.bfloat16)
        scaled_out = (scale_out[:, None] * hidden_wide).astype(jnp.bfloat16)
        summed_direct, summed_reverse = forward_messages(scaled_in, scaled_out)
        msg_in = (scale_out[:, None] * summed_direct).astype(jnp.bfloat16)
        msg_out = (scale_in[:, None] * summed_reverse).astype(jnp.bfloat16)
        preact = jnp.dot(msg_in, weight_in[layer], preferred_element_type=jnp.float32)
        preact = preact + jnp.dot(msg_out, weight_out[layer], preferred_element_type=jnp.float32)
        preact = preact + jnp.dot(hidden, weight_self[layer], preferred_element_type=jnp.float32)
        preact = preact + layer_bias[layer][None, :]
        stored.append((hidden, msg_in, msg_out, preact))
        hidden = activation(preact).astype(jnp.bfloat16)
    out_features = hidden
    upstream = cotangent.astype(jnp.float32)
    ones = jnp.ones((features.shape[0], 8), jnp.bfloat16)
    grads = []
    for layer in reversed(range(layer_total)):
        hidden, msg_in, msg_out, preact = stored[layer]
        unused, pullback = jax.vjp(activation, preact)
        grad_z = pullback(upstream)[0].astype(jnp.bfloat16)
        parts = jnp.concatenate([msg_in, msg_out, hidden, ones], axis=1)
        grads.append(jnp.einsum("nf,ng->fg", parts, grad_z, preferred_element_type=jnp.float32))
        back_in = (
            scale_out[:, None]
            * jnp.dot(grad_z, weight_in[layer].T, preferred_element_type=jnp.float32)
        ).astype(jnp.bfloat16)
        back_out = (
            scale_in[:, None]
            * jnp.dot(grad_z, weight_out[layer].T, preferred_element_type=jnp.float32)
        ).astype(jnp.bfloat16)
        backward_summed_direct, backward_summed_reverse = forward_messages(back_out, back_in)
        upstream = (
            scale_out[:, None] * backward_summed_direct
            + scale_in[:, None] * backward_summed_reverse
        )
        upstream = upstream + jnp.dot(
            grad_z, weight_self[layer].T, preferred_element_type=jnp.float32
        )
    total = lax.psum(jnp.stack(grads[::-1]), ("row", "col"))
    width = features.shape[1]
    return (
        out_features,
        upstream,
        total[:, :width],
        total[:, width : 2 * width],
        total[:, 2 * width : 3 * width],
        total[:, 3 * width],
    )


def solution(mesh):
    return jax.shard_map(
        per_device,
        mesh=mesh,
        in_specs=(
            P(("row", "col"), None),
            P(),
            P(),
            P(),
            P(),
            P(("row", "col")),
            P(("row", "col")),
            P(("row", "col"), None, None),
            P(("row", "col")),
            P(("row", "col")),
            P(("row", "col"), None),
        ),
        out_specs=(P(("row", "col"), None), P(("row", "col"), None), P(), P(), P(), P()),
        check_vma=False,
    )
```

time: 665 us -> 547 us (0.82); the launches traced: 658 us -> 547 us
  matrix products: 152 us -> 46.6 us
  waiting for transfers between devices: 339 us -> 411 us
  blocking collectives: 117 us -> 47 us
  local copies, waits for them, and re-layouts: 25.6 us -> 10.4 us
  other arithmetic: 6.31 us -> 16.6 us
    dot_general x54 -> x10, matrix products: 140 us -> 39 us  [the longest x4 19.5 us: forward_messages(): lax.dot_general(block, row_rows, (((0,), (0,)), ((), ())), preferred_elem...]
    psum x1, waiting for transfers between devices: 24.9 us -> 116 us  [per_device(): total = lax.psum(jnp.stack(grads[::-1]), ('row', 'col'))]
    psum x1 -> x0, blocking collectives: 74.3 us -> none  [per_device(): lax.psum((local_grads[0], local_grads[1], local_grads[2], local_grads[3])...]
    all_gather x4, waiting for transfers between devices: 39.7 us -> 73.2 us  [forward_messages(): column_rows = lax.all_gather(first, 'row', axis=0, tiled=True)]
    reduce_scatter x4, waiting for transfers between devices: 175 us -> 147 us  [forward_messages(): lax.psum_scatter(reverse, 'row', scatter_dimension=0, tiled=True)]
    reduce_scatter x4, waiting for transfers between devices: 99.1 us -> 74.4 us  [forward_messages(): lax.psum_scatter(direct, 'col', scatter_dimension=0, tiled=True)]
    while x8 -> x0, local copies, waits for them, and re-layouts: 15.4 us -> none  [tile_product(): running = lax.fori_loop(0, turn_count, add_group, start_value)]
    convert_element_type x1 -> x6, other arithmetic: 0.76 us -> 11.1 us  [the longest x2 6.23 us: dense_block(): cols.append(total.astype(jnp.bfloat16))]
  transfers between devices with their start and end apart: 13 -> 13, of which waited for: 13 -> 13; matrix products, arithmetic and copies ran while one was open for 17% -> 7% of each run, Pallas kernels for 0% -> 0%
where the time goes in v1:
time: 547 us
  waiting for transfers between devices  411 us (75%)
  blocking collectives  47 us (9%)
  matrix products  46.6 us (9%)
  other arithmetic  16.6 us (3%)
  between operations  14.8 us (3%)
  local copies, waits for them, and re-layouts  10.4 us (2%)
    reduce_scatter x4, waiting for transfers between devices, forward_messages(): lax.psum_scatter(reverse, 'row', scatter_dimension=0, tiled=True)  147 us
    psum x1, waiting for transfers between devices, per_device(): total = lax.psum(jnp.stack(grads[::-1]), ('row', 'col'))  116 us
    reduce_scatter x4, waiting for transfers between devices, forward_messages(): lax.psum_scatter(direct, 'col', scatter_dimension=0, tiled=True)  74.4 us
    all_gather x4, waiting for transfers between devices, forward_messages(): column_rows = lax.all_gather(first, 'row', axis=0, tiled=True)  73.2 us
    all_gather x4, blocking collectives, forward_messages(): row_rows = lax.all_gather(second, 'col', axis=0, tiled=True)  47 us
    dot_general x4, matrix products, forward_messages(): lax.dot_general(block, row_rows, (((0,), (0,)), ((), ())), preferred_elem...  19.5 us
    dot_general x4, matrix products, forward_messages(): direct = jnp.dot(block, column_rows, preferred_element_type=jnp.float32)  18.9 us
  transfers between devices with their start and end apart: 13, of which 13 were waited for; matrix products, arithmetic and copies ran while one was open for 7% of the time, Pallas kernels for 0%

profile of v1, /device:TPU:0, one launch (start us, length us, event | category | flops | bytes accessed | tf_op | source)
XLA Modules:
  0.0 546.8 jit_solution(5448452472395076032)
XLA Ops:
  7.2 0.7 convert_rsqrt_fusion
  7.9 1.7 fusion.35
  10.3 0.7 compare_select_fusion
  11.1 0.4 compare_reduce_fusion.15
  11.5 3.9 fusion.3
  15.5 2.3 fusion.7
  17.8 0.6 maximum_maximum_fusion
  18.4 2.5 copy.36
  20.9 3.4 copy.47
  24.3 10.9 %all-gather.5.cloned.1.call-done = bf16[2048,256]{1,0:T(8,128)(2,1)} async-done(((bf16[256,256]{1,0:T(8,128)(2,1)}), bf16[2048,256]{1,0:T(8,128)(2,1)}) %all-gather.5.cloned.1.call-update) | async-done | bytes 1048592 | tf_op jit(solution)/shard_map/all_gather | solution.py:57
  35.1 4.7 fusion.87
  40.0 12.7 %all_gather.25 = bf16[1024,256]{1,0:T(8,128)(2,1)S(1)} all-gather(bf16[256,256]{1,0:T(8,128)(2,1)S(1)} %get-tuple-element.33), channel_id=1, replica_groups=mesh['row'=8,'col'=4] {'col'}, dimensions={0}, use_global_device_ids=true | all-gather | bytes 655360 | tf_op jit(solution)/shard_map/all_gather | solution.py:56
  52.7 4.9 fusion.88
  57.7 0.6 copy-done.5
  58.3 9.6 %reduce-scatter.9.cloned.1.call-done = f32[256,256]{1,0:T(8,128)} async-done(((f32[1024,256]{1,0:T(8,128)}), f32[256,256]{1,0:T(8,128)}) %reduce-scatter.9.cloned.1.call-update) | async-done | bytes 262160 | tf_op jit(solution)/shard_map/reduce_scatter | solution.py:63
  67.9 1.0 multiply_convert_fusion.5
  69.1 37.1 %reduce-scatter.11.cloned.1.call-done = f32[256,256]{1,0:T(8,128)} async-done(((f32[2048,256]{1,0:T(8,128)}), f32[256,256]{1,0:T(8,128)}) %reduce-scatter.11.cloned.1.call-update) | async-done | bytes 262160 | tf_op jit(solution)/shard_map/reduce_scatter | solution.py:62
  106.3 1.0 multiply_convert_fusion.4
  107.8 10.5 %all_gather.27 = bf16[1024,256]{1,0:T(8,128)(2,1)S(1)} all-gather(bf16[256,256]{1,0:T(8,128)(2,1)S(1)} %get-tuple-element.22), channel_id=1, replica_groups=mesh['row'=8,'col'=4] {'col'}, dimensions={0}, use_global_device_ids=true | all-gather | bytes 655360 | tf_op jit(solution)/shard_map/all_gather | solution.py:56
  118.3 4.8 fusion.90
  123.2 33.3 %reduce-scatter.15.cloned.1.call-done = f32[256,256]{1,0:T(8,128)} async-done(((f32[2048,256]{1,0:T(8,128)}), f32[256,256]{1,0:T(8,128)}) %reduce-scatter.15.cloned.1.call-update) | async-done | bytes 262160 | tf_op jit(solution)/shard_map/reduce_scatter | solution.py:62
  156.6 1.7 multiply_convert_fusion.1
  158.4 21.1 %all-gather.7.cloned.1.call-done = bf16[2048,256]{1,0:T(8,128)(2,1)} async-done(((bf16[256,256]{1,0:T(8,128)(2,1)}), bf16[2048,256]{1,0:T(8,128)(2,1)}) %all-gather.7.cloned.1.call-update) | async-done | bytes 1048592 | tf_op jit(solution)/shard_map/all_gather | solution.py:57
  179.5 4.7 fusion.89
  184.3 27.6 %reduce-scatter.13.cloned.1.call-done = f32[256,256]{1,0:T(8,128)} async-done(((f32[1024,256]{1,0:T(8,128)}), f32[256,256]{1,0:T(8,128)}) %reduce-scatter.13.cloned.1.call-update) | async-done | bytes 262160 | tf_op jit(solution)/shard_map/reduce_scatter | solution.py:63
  211.9 1.0 multiply_convert_fusion.2
  213.4 1.0 fusion.40
  214.4 0.9 fusion.18
  215.4 22.3 %all-gather.9.cloned.1.call-done = bf16[2048,256]{1,0:T(8,128)(2,1)} async-done(((bf16[256,256]{1,0:T(8,128)(2,1)}), bf16[2048,256]{1,0:T(8,128)(2,1)}) %all-gather.9.cloned.1.call-update) | async-done | bytes 1048592 | tf_op jit(solution)/shard_map/all_gather | solution.py:57
  237.7 4.7 fusion.91
  242.7 12.8 %all_gather.29 = bf16[1024,256]{1,0:T(8,128)(2,1)S(1)} all-gather(bf16[256,256]{1,0:T(8,128)(2,1)S(1)} %fusion.19), channel_id=1, replica_groups=mesh['row'=8,'col'=4] {'col'}, dimensions={0}, use_global_device_ids=true | all-gather | bytes 655360 | tf_op jit(solution)/shard_map/all_gather | solution.py:56
  255.5 4.9 fusion.92
  260.5 10.1 %reduce-scatter.17.cloned.1.call-done = f32[256,256]{1,0:T(8,128)} async-done(((f32[1024,256]{1,0:T(8,128)}), f32[256,256]{1,0:T(8,128)}) %reduce-scatter.17.cloned.1.call-update) | async-done | bytes 262160 | tf_op jit(solution)/shard_map/reduce_scatter | solution.py:63
  270.6 38.4 %reduce-scatter.19.cloned.1.call-done = f32[256,256]{1,0:T(8,128)} async-done(((f32[2048,256]{1,0:T(8,128)}), f32[256,256]{1,0:T(8,128)}) %reduce-scatter.19.cloned.1.call-update) | async-done | bytes 262160 | tf_op jit(solution)/shard_map/reduce_scatter | solution.py:62
  308.9 1.4 fusion.49
  310.3 0.9 fusion.20
  311.9 1.4 pad_maximum_fusion
  313.3 18.8 %all-gather.11.cloned.1.call-done = bf16[2048,256]{1,0:T(8,128)(2,1)} async-done(((bf16[256,256]{1,0:T(8,128)(2,1)}), bf16[2048,256]{1,0:T(8,128)(2,1)}) %all-gather.11.cloned.1.call-update) | async-done | bytes 1048592 | tf_op jit(solution)/shard_map/all_gather | solution.py:57
  332.2 4.7 fusion.93
  337.2 11.1 %all_gather.31 = bf16[1024,256]{1,0:T(8,128)(2,1)S(1)} all-gather(bf16[256,256]{1,0:T(8,128)(2,1)S(1)} %fusion.21), channel_id=1, replica_groups=mesh['row'=8,'col'=4] {'col'}, dimensions={0}, use_global_device_ids=true | all-gather | bytes 655360 | tf_op jit(solution)/shard_map/all_gather | solution.py:56
  348.3 4.8 fusion.94
  353.1 116.1 %all-reduce.2.cloned.1.call-done = f32[2,776,256]{2,1,0:T(8,128)} async-done(((f32[2,776,256]{2,1,0:T(8,128)}), f32[2,776,256]{2,1,0:T(8,128)}) %all-reduce.2.cloned.1.call-update) | async-done | bytes 1589264 | tf_op jit(solution)/shard_map/psum | solution.py:108
  469.3 0.7 slice.121
  470.0 0.6 copy.49
  470.6 2.5 fusion.85
  473.1 27.0 %reduce-scatter.21.cloned.1.call-done = f32[256,256]{1,0:T(8,128)} async-done(((f32[1024,256]{1,0:T(8,128)}), f32[256,256]{1,0:T(8,128)}) %reduce-scatter.21.cloned.1.call-update) | async-done | bytes 262160 | tf_op jit(solution)/shard_map/reduce_scatter | solution.py:63
  500.1 38.2 %reduce-scatter.23.cloned.1.call-done = f32[256,256]{1,0:T(8,128)} async-done(((f32[2048,256]{1,0:T(8,128)}), f32[256,256]{1,0:T(8,128)}) %reduce-scatter.23.cloned.1.call-update) | async-done | bytes 262160 | tf_op jit(solution)/shard_map/reduce_scatter | solution.py:62
  538.3 2.0 convolution_add_fusion
  (52 shorter events, 3.0 us)
Async XLA Ops:
  7.2 28.0 %all-gather.5.cloned.1.call-start = ((), (), s32[]{:S(2)}) async-start(), calls=%async_computation.8 | async-start | bytes 1179648 | tf_op jit(solution)/shard_map/all_gather | solution.py:57
  9.6 58.3 %reduce-scatter.9.cloned.1.call-start = ((), (), s32[]{:S(2)}) async-start(), calls=%async_computation.9 | async-start | bytes 1310720 | tf_op jit(solution)/shard_map/reduce_scatter | solution.py:63
  11.5 4.0 copy-start
  39.9 66.4 %reduce-scatter.11.cloned.1.call-start = ((), (), s32[]{:S(2)}) async-start(), calls=%async_computation.10 | async-start | bytes 2359296 | tf_op jit(solution)/shard_map/reduce_scatter | solution.py:62
  57.6 0.7 copy-start.5
  57.6 11.4 %copy-start.2 = (bf16[2,256,256]{2,1,0:T(8,128)(2,1)S(1)}, bf16[2,256,256]{2,1,0:T(8,128)(2,1)}, u32[]{:S(2)}) copy-start(bf16[2,256,256]{2,1,0:T(8,128)(2,1)} %param.12) | copy-start | bytes 786436
  57.6 49.7 %copy-start.1 = (bf16[2,256,256]{2,1,0:T(8,128)(2,1)S(1)}, bf16[2,256,256]{2,1,0:T(8,128)(2,1)}, u32[]{:S(2)}) copy-start(bf16[2,256,256]{2,1,0:T(8,128)(2,1)} %param.13) | copy-start | bytes 786436
  57.6 49.9 %copy-start.3 = (bf16[256,256]{1,0:T(8,128)(2,1)S(1)}, bf16[256,256]{1,0:T(8,128)(2,1)}, u32[]{:S(2)}) copy-start(bf16[256,256]{1,0:T(8,128)(2,1)} %param.11) | copy-start | bytes 393220
  57.6 49.9 %copy-start.4 = (bf16[2,256,256]{2,1,0:T(8,128)(2,1)S(1)}, bf16[2,256,256]{2,1,0:T(8,128)(2,1)}, u32[]{:S(2)}) copy-start(bf16[2,256,256]{2,1,0:T(8,128)(2,1)} %param.14) | copy-start | bytes 786436
  57.6 98.9 %reduce-scatter.15.cloned.1.call-start = ((), (), s32[]{:S(2)}) async-start(), calls=%async_computation.13 | async-start | bytes 2359296 | tf_op jit(solution)/shard_map/reduce_scatter | solution.py:62
  123.2 56.3 %all-gather.7.cloned.1.call-start = ((), (), s32[]{:S(2)}) async-start(), calls=%async_computation.11 | async-start | bytes 1179648 | tf_op jit(solution)/shard_map/all_gather | solution.py:57
  158.3 53.6 %reduce-scatter.13.cloned.1.call-start = ((), (), s32[]{:S(2)}) async-start(), calls=%async_computation.12 | async-start | bytes 1310720 | tf_op jit(solution)/shard_map/reduce_scatter | solution.py:63
  184.2 29.2 %copy-start.6 = (bf16[256,256]{1,0:T(8,128)(2,1)S(1)}, bf16[256,256]{1,0:T(8,128)(2,1)}, u32[]{:S(2)}) copy-start(bf16[256,256]{1,0:T(8,128)(2,1)} %param.21) | copy-start | bytes 393220
  184.2 53.5 %all-gather.9.cloned.1.call-start = ((), (), s32[]{:S(2)}) async-start(), calls=%async_computation.14 | async-start | bytes 1179648 | tf_op jit(solution)/shard_map/all_gather | solution.py:57
  215.3 55.3 %reduce-scatter.17.cloned.1.call-start = ((), (), s32[]{:S(2)}) async-start(), calls=%async_computation.15 | async-start | bytes 1310720 | tf_op jit(solution)/shard_map/reduce_scatter | solution.py:63
  242.5 66.5 %reduce-scatter.19.cloned.1.call-start = ((), (), s32[]{:S(2)}) async-start(), calls=%async_computation.16 | async-start | bytes 2359296 | tf_op jit(solution)/shard_map/reduce_scatter | solution.py:62
  260.4 71.8 %all-gather.11.cloned.1.call-start = ((), (), s32[]{:S(2)}) async-start(), calls=%async_computation.17 | async-start | bytes 1179648 | tf_op jit(solution)/shard_map/all_gather | solution.py:57
  311.2 158.1 %all-reduce.2.cloned.1.call-start = ((), (), s32[]{:S(2)}) async-start(), calls=%async_computation.20 | async-start | bytes 3178496 | tf_op jit(solution)/shard_map/psum | solution.py:108
  313.3 186.8 %reduce-scatter.21.cloned.1.call-start = ((), (), s32[]{:S(2)}) async-start(), calls=%async_computation.18 | async-start | bytes 1310720 | tf_op jit(solution)/shard_map/reduce_scatter | solution.py:63
  336.9 201.4 %reduce-scatter.23.cloned.1.call-start = ((), (), s32[]{:S(2)}) async-start(), calls=%async_computation.19 | async-start | bytes 2359296 | tf_op jit(solution)/shard_map/reduce_scatter | solution.py:62
Sparse Core Ops, SparseCore 0:
  10.1 24.9 all-gather.4
  40.0 27.8 reduce-scatter.8
  70.2 36.0 reduce-scatter.10
  123.3 33.2 reduce-scatter.14
  158.6 20.8 all-gather.6
  184.3 27.5 reduce-scatter.12
  215.4 22.2 all-gather.8
  242.6 27.9 reduce-scatter.16
  272.9 36.0 reduce-scatter.18
  311.3 20.8 all-gather.10
  337.6 131.6 all-reduce.1
  472.0 28.0 reduce-scatter.20
  502.4 35.8 reduce-scatter.22

commit v2 on v1

--- a/solution.py
+++ b/solution.py
@@ -60,7 +60,9 @@
         )
         direct = jnp.dot(block, column_rows, preferred_element_type=jnp.float32)
         summed_reverse = lax.psum_scatter(reverse, "row", scatter_dimension=0, tiled=True)
-        summed_direct = lax.psum_scatter(direct, "col", scatter_dimension=0, tiled=True)
+        pieces = direct.astype(jnp.bfloat16).reshape((lax.axis_size("col"), -1, direct.shape[1]))
+        pieces = lax.all_to_all(pieces, "col", 0, 0, tiled=True)
+        summed_direct = jnp.sum(pieces.astype(jnp.float32), axis=0)
         return (summed_direct, summed_reverse)
 
     layer_total = weight_in.shape[0]
@@ -81,7 +83,7 @@
         hidden = activation(preact).astype(jnp.bfloat16)
     out_features = hidden
     upstream = cotangent.astype(jnp.float32)
-    ones = jnp.ones((features.shape[0], 8), jnp.bfloat16)
+    ones = jnp.ones((features.shape[0], 256), jnp.bfloat16)
     grads = []
     for layer in reversed(range(layer_total)):
         hidden, msg_in, msg_out, preact = stored[layer]
@@ -105,8 +107,12 @@
         upstream = upstream + jnp.dot(
             grad_z, weight_self[layer].T, preferred_element_type=jnp.float32
         )
-    total = lax.psum(jnp.stack(grads[::-1]), ("row", "col"))
     width = features.shape[1]
+    total = jnp.concatenate(grads[::-1], axis=0)
+    total = lax.psum_scatter(total, "row", scatter_dimension=0, tiled=True)
+    total = lax.psum_scatter(total, "col", scatter_dimension=0, tiled=True)
+    total = lax.all_gather(total, ("row", "col"), axis=0, tiled=True)
+    total = total.reshape(layer_total, -1, width)
     return (
         out_features,
         upstream,

time: 547 us -> 430 us (0.79)
  waiting for transfers between devices: 411 us -> 280 us
  starting transfers between devices: 0.54 us -> 14.7 us
    psum x1 -> x0, waiting for transfers between devices: 116 us -> none  [per_device(): total = lax.psum(jnp.stack(grads[::-1]), ('row', 'col'))]
    all_gather x0 -> x1, waiting for transfers between devices: none -> 55.8 us  [per_device(): total = lax.all_gather(total, ('row', 'col'), axis=0, tiled=True)]
    reduce_scatter x4, waiting for transfers between devices: 147 us -> 96.2 us  [forward_messages(): lax.psum_scatter(reverse, 'row', scatter_dimension=0, tiled=True)]
    reduce_scatter x4 -> x2, waiting for transfers between devices: 74.4 us -> 41.5 us  [the longest x1 34.5 us: per_device(): total = lax.psum_scatter(total, 'row', scatter_dimension=0, tiled=True)]
    all_to_all x0 -> x4, waiting for transfers between devices: none -> 31.5 us  [forward_messages(): pieces = lax.all_to_all(pieces, 'col', 0, 0, tiled=True)]
    all_gather x4, waiting for transfers between devices: 73.2 us -> 54.6 us  [forward_messages(): column_rows = lax.all_gather(first, 'row', axis=0, tiled=True)]
    all_to_all x0 -> x4, starting transfers between devices: none -> 14 us  [forward_messages(): pieces = lax.all_to_all(pieces, 'col', 0, 0, tiled=True)]
  transfers between devices with their start and end apart: 13 -> 15, of which waited for: 13 -> 14; matrix products, arithmetic and copies ran while one was open for 7% -> 10% of each run, Pallas kernels for 0% -> 0%
where the time goes in v2:
time: 430 us
  waiting for transfers between devices  280 us (65%)
  blocking collectives  52.4 us (12%)
  matrix products  42.9 us (10%)
  between operations  14.9 us (3%)
  starting transfers between devices  14.7 us (3%)
  other arithmetic  13.8 us (3%)
  local copies, waits for them, and re-layouts  11.1 us (3%)
    reduce_scatter x4, waiting for transfers between devices, forward_messages(): lax.psum_scatter(reverse, 'row', scatter_dimension=0, tiled=True)  96.2 us
    all_gather x1, waiting for transfers between devices, per_device(): total = lax.all_gather(total, ('row', 'col'), axis=0, tiled=True)  55.8 us
    all_gather x4, waiting for transfers between devices, forward_messages(): column_rows = lax.all_gather(first, 'row', axis=0, tiled=True)  54.6 us
    all_gather x4, blocking collectives, forward_messages(): row_rows = lax.all_gather(second, 'col', axis=0, tiled=True)  52.4 us
    reduce_scatter x1, waiting for transfers between devices, per_device(): total = lax.psum_scatter(total, 'row', scatter_dimension=0, tiled=True)  34.5 us
    all_to_all x4, waiting for transfers between devices, forward_messages(): pieces = lax.all_to_all(pieces, 'col', 0, 0, tiled=True)  31.5 us
    dot_general x4, matrix products, forward_messages(): direct = jnp.dot(block, column_rows, preferred_element_type=jnp.float32)  18.3 us
    dot_general x4, matrix products, forward_messages(): lax.dot_general(block, row_rows, (((0,), (0,)), ((), ())), preferred_elem...  17.1 us
  transfers between devices with their start and end apart: 15, of which 14 were waited for; matrix products, arithmetic and copies ran while one was open for 10% of the time, Pallas kernels for 0%

profile of v2, /device:TPU:0, one launch (start us, length us, event | category | flops | bytes accessed | tf_op | source)
XLA Modules:
  0.0 429.6 jit_solution(17725921120352170777)
XLA Ops:
  7.2 1.0 copy.100
  8.2 0.7 convert_rsqrt_fusion
  11.5 3.9 fusion.3
  15.5 2.3 fusion.7
  18.5 2.4 copy.99
  20.9 1.5 copy.140
  22.4 15.1 %all_gather.28 = bf16[1024,256]{0,1:T(8,128)(2,1)S(1)} all-gather(bf16[256,256]{0,1:T(8,128)(2,1)S(1)} %get-tuple-element.63), channel_id=1, replica_groups=mesh['row'=8,'col'=4] {'col'}, dimensions={0}, use_global_device_ids=true | all-gather | bytes 655360 | tf_op jit(solution)/shard_map/all_gather | solution.py:56
  37.5 2.6 fusion.89
  40.2 4.6 %convolution_convert_fusion.3 = bf16[1024,256]{1,0:T(8,128)(2,1)} fusion(bf16[1024,2048]{1,0:T(8,128)(2,1)} %bitcast.138, bf16[2048,256]{0,1:T(8,128)(2,1)} %all-gather.6.cloned.1.call-done), kind=kOutput, calls=%fused_computation.37 | convolution fusion | flops 1074003968 | bytes 5767168 | tf_op jit(solution)/shard_map/dot_general | solution.py:61
  44.7 3.6 all-to-all-start
  48.4 6.9 %all-to-all-done = bf16[4,256,256]{2,1,0:T(8,128)(2,1)S(1)} async-done(((bf16[4,256,256]{2,1,0:T(8,128)(2,1)}), bf16[4,256,256]{2,1,0:T(8,128)(2,1)S(1)}, u32[]{:S(2)}, u32[]{:S(2)}) %all-to-all-start) | async-done | bytes 524320 | tf_op jit(solution)/shard_map/all_to_all | solution.py:64
  55.8 20.6 %reduce-scatter.7.cloned.1.call-done = f32[256,256]{0,1:T(8,128)} async-done(((f32[2048,256]{0,1:T(8,128)}), f32[256,256]{0,1:T(8,128)}) %reduce-scatter.7.cloned.1.call-update) | async-done | bytes 262160 | tf_op jit(solution)/shard_map/reduce_scatter | solution.py:62
  76.4 1.0 multiply_convert_fusion.4
  77.7 1.0 fusion.39
  78.7 12.2 %all_gather.30 = bf16[1024,256]{0,1:T(8,128)(2,1)S(1)} all-gather(bf16[256,256]{0,1:T(8,128)(2,1)S(1)} %get-tuple-element.52), channel_id=1, replica_groups=mesh['row'=8,'col'=4] {'col'}, dimensions={0}, use_global_device_ids=true | all-gather | bytes 655360 | tf_op jit(solution)/shard_map/all_gather | solution.py:56
  90.9 4.8 %fusion.90 = f32[2048,256]{0,1:T(8,128)} fusion(bf16[1024,256]{0,1:T(8,128)(2,1)S(1)} %all_gather.30, bf16[1024,2048]{1,0:T(8,128)(2,1)} %bitcast.139), kind=kOutput, calls=%fused_computation.166 | convolution fusion | flops 1073741824 | bytes 6815744 | tf_op jit(solution)/shard_map/dot_general | solution.py:58
  95.9 35.4 %reduce-scatter.9.cloned.1.call-done = f32[256,256]{0,1:T(8,128)} async-done(((f32[2048,256]{0,1:T(8,128)}), f32[256,256]{0,1:T(8,128)}) %reduce-scatter.9.cloned.1.call-update) | async-done | bytes 262160 | tf_op jit(solution)/shard_map/reduce_scatter | solution.py:62
  131.4 1.7 multiply_convert_fusion.1
  133.1 22.9 %all-gather.8.cloned.1.call-done = bf16[2048,256]{0,1:T(8,128)(2,1)} async-done(((bf16[256,256]{0,1:T(8,128)(2,1)}), bf16[2048,256]{0,1:T(8,128)(2,1)}) %all-gather.8.cloned.1.call-update) | async-done | bytes 1048592 | tf_op jit(solution)/shard_map/all_gather | solution.py:57
  156.0 4.6 %convolution_convert_fusion.2 = bf16[1024,256]{1,0:T(8,128)(2,1)} fusion(bf16[1024,2048]{1,0:T(8,128)(2,1)} %bitcast.140, bf16[2048,256]{0,1:T(8,128)(2,1)} %all-gather.8.cloned.1.call-done), kind=kOutput, calls=%fused_computation.36 | convolution fusion | flops 1074003968 | bytes 5767168 | tf_op jit(solution)/shard_map/dot_general | solution.py:61
  160.6 3.5 all-to-all-start.1
  164.2 8.5 %all-to-all-done.1 = bf16[4,256,256]{2,1,0:T(8,128)(2,1)S(1)} async-done(((bf16[4,256,256]{2,1,0:T(8,128)(2,1)}), bf16[4,256,256]{2,1,0:T(8,128)(2,1)S(1)}, u32[]{:S(2)}, u32[]{:S(2)}) %all-to-all-start.1) | async-done | bytes 524320 | tf_op jit(solution)/shard_map/all_to_all | solution.py:64
  173.8 0.8 fusion.18
  175.0 12.4 %all_gather.32 = bf16[1024,256]{0,1:T(8,128)(2,1)S(1)} all-gather(bf16[256,256]{0,1:T(8,128)(2,1)S(1)} %fusion.19), channel_id=1, replica_groups=mesh['row'=8,'col'=4] {'col'}, dimensions={0}, use_global_device_ids=true | all-gather | bytes 655360 | tf_op jit(solution)/shard_map/all_gather | solution.py:56
  187.4 4.8 %fusion.91 = f32[2048,256]{0,1:T(8,128)} fusion(bf16[1024,256]{0,1:T(8,128)(2,1)S(1)} %all_gather.32, bf16[1024,2048]{1,0:T(8,128)(2,1)} %bitcast.141), kind=kOutput, calls=%fused_computation.167 | convolution fusion | flops 1073741824 | bytes 6815744 | tf_op jit(solution)/shard_map/dot_general | solution.py:58
  192.3 5.5 %all-gather.10.cloned.1.call-done = bf16[2048,256]{0,1:T(8,128)(2,1)} async-done(((bf16[256,256]{0,1:T(8,128)(2,1)}), bf16[2048,256]{0,1:T(8,128)(2,1)}) %all-gather.10.cloned.1.call-update) | async-done | bytes 1048592 | tf_op jit(solution)/shard_map/all_gather | solution.py:57
  197.8 4.6 %convolution_convert_fusion.1 = bf16[1024,256]{1,0:T(8,128)(2,1)} fusion(bf16[1024,2048]{1,0:T(8,128)(2,1)} %bitcast.142, bf16[2048,256]{0,1:T(8,128)(2,1)} %all-gather.10.cloned.1.call-done), kind=kOutput, calls=%fused_computation.35 | convolution fusion | flops 1074003968 | bytes 5767168 | tf_op jit(solution)/shard_map/dot_general | solution.py:61
  202.4 3.5 all-to-all-start.2
  206.3 8.2 %all-to-all-done.2 = bf16[4,256,256]{2,1,0:T(8,128)(2,1)S(1)} async-done(((bf16[4,256,256]{2,1,0:T(8,128)(2,1)}), bf16[4,256,256]{2,1,0:T(8,128)(2,1)S(1)}, u32[]{:S(2)}, u32[]{:S(2)}) %all-to-all-start.2) | async-done | bytes 524320 | tf_op jit(solution)/shard_map/all_to_all | solution.py:64
  214.7 20.1 %reduce-scatter.11.cloned.1.call-done = f32[256,256]{0,1:T(8,128)} async-done(((f32[2048,256]{0,1:T(8,128)}), f32[256,256]{0,1:T(8,128)}) %reduce-scatter.11.cloned.1.call-update) | async-done | bytes 262160 | tf_op jit(solution)/shard_map/reduce_scatter | solution.py:62
  234.8 1.3 fusion.51
  236.5 1.5 pad_maximum_fusion
  238.1 34.5 %reduce-scatter.15.cloned.1.call-done = f32[256,256]{1,0:T(8,128)} async-done(((f32[2048,256]{1,0:T(8,128)}), f32[256,256]{1,0:T(8,128)}) %reduce-scatter.15.cloned.1.call-update) | async-done | bytes 262160 | tf_op jit(solution)/shard_map/reduce_scatter | solution.py:112
  272.6 0.8 fusion.20
  273.8 12.7 %all_gather.34 = bf16[1024,256]{0,1:T(8,128)(2,1)S(1)} all-gather(bf16[256,256]{0,1:T(8,128)(2,1)S(1)} %fusion.21), channel_id=1, replica_groups=mesh['row'=8,'col'=4] {'col'}, dimensions={0}, use_global_device_ids=true | all-gather | bytes 655360 | tf_op jit(solution)/shard_map/all_gather | solution.py:56
  286.4 4.8 %fusion.92 = f32[2048,256]{0,1:T(8,128)} fusion(bf16[1024,256]{0,1:T(8,128)(2,1)S(1)} %all_gather.34, bf16[1024,2048]{1,0:T(8,128)(2,1)} %bitcast.143), kind=kOutput, calls=%fused_computation.168 | convolution fusion | flops 1073741824 | bytes 6815744 | tf_op jit(solution)/shard_map/dot_general | solution.py:58
  291.3 7.0 %reduce-scatter.17.cloned.1.call-done = f32[64,256]{1,0:T(8,128)} async-done(((f32[256,256]{1,0:T(8,128)}), f32[64,256]{1,0:T(8,128)}) %reduce-scatter.17.cloned.1.call-update) | async-done | bytes 65552 | tf_op jit(solution)/shard_map/reduce_scatter | solution.py:113
  298.4 26.1 %all-gather.12.cloned.1.call-done = bf16[2048,256]{0,1:T(8,128)(2,1)} async-done(((bf16[256,256]{0,1:T(8,128)(2,1)}), bf16[2048,256]{0,1:T(8,128)(2,1)}) %all-gather.12.cloned.1.call-update) | async-done | bytes 1048592 | tf_op jit(solution)/shard_map/all_gather | solution.py:57
  324.4 4.6 %convolution_convert_fusion = bf16[1024,256]{1,0:T(8,128)(2,1)} fusion(bf16[1024,2048]{1,0:T(8,128)(2,1)} %bitcast.144, bf16[2048,256]{0,1:T(8,128)(2,1)} %all-gather.12.cloned.1.call-done), kind=kOutput, calls=%fused_computation.34 | convolution fusion | flops 1074003968 | bytes 5767168 | tf_op jit(solution)/shard_map/dot_general | solution.py:61
  329.0 3.5 all-to-all-start.3
  332.5 0.8 copy.121
  333.2 7.9 %all-to-all-done.3 = bf16[4,256,256]{2,1,0:T(8,128)(2,1)S(1)} async-done(((bf16[4,256,256]{2,1,0:T(8,128)(2,1)}), bf16[4,256,256]{2,1,0:T(8,128)(2,1)S(1)}, u32[]{:S(2)}, u32[]{:S(2)}) %all-to-all-start.3) | async-done | bytes 524320 | tf_op jit(solution)/shard_map/all_to_all | solution.py:64
  341.4 20.1 %reduce-scatter.13.cloned.1.call-done = f32[256,256]{0,1:T(8,128)} async-done(((f32[2048,256]{0,1:T(8,128)}), f32[256,256]{0,1:T(8,128)}) %reduce-scatter.13.cloned.1.call-update) | async-done | bytes 262160 | tf_op jit(solution)/shard_map/reduce_scatter | solution.py:62
  361.4 1.1 convolution_add_fusion
  362.6 0.8 copy.122
  363.4 55.8 %all-gather.14.cloned.1.call-done = f32[2048,256]{1,0:T(8,128)} async-done(((f32[64,256]{1,0:T(8,128)}), f32[2048,256]{1,0:T(8,128)}) %all-gather.14.cloned.1.call-update) | async-done | bytes 2097168 | tf_op jit(solution)/shard_map/all_gather | solution.py:114
  419.2 2.5 fusion.87
  421.7 0.7 slice.121
  (68 shorter events, 7.3 us)
Async XLA Ops:
  7.2 33.0 %all-gather.6.cloned.1.call-start = ((), (), s32[]{:S(2)}) async-start(), calls=%async_computation.10 | async-start | bytes 1179648 | tf_op jit(solution)/shard_map/all_gather | solution.py:57
  9.7 66.8 %reduce-scatter.7.cloned.1.call-start = ((), (), s32[]{:S(2)}) async-start(), calls=%async_computation.11 | async-start | bytes 2359296 | tf_op jit(solution)/shard_map/reduce_scatter | solution.py:62
  11.5 4.0 copy-start
  22.4 15.1 %copy-start.1 = (bf16[128,8,8,256]{3,1,2,0:T(8,128)(2,1)}, bf16[128,8,8,256]{3,1,2,0:T(8,128)(2,1)S(1)}, u32[]{:S(2)}) copy-start(bf16[128,8,8,256]{3,1,2,0:T(8,128)(2,1)S(1)} %copy.140) | copy-start | bytes 12582916
  40.1 8.3 %copy-start.7 = (f32[2,256]{1,0:T(2,128)S(1)}, f32[2,256]{1,0:T(2,128)}, u32[]{:S(2)}) copy-start(f32[2,256]{1,0:T(2,128)} %param.15) | copy-start | bytes 6148
  44.7 10.8 %copy-start.3 = (bf16[2,256,256]{2,1,0:T(8,128)(2,1)S(1)}, bf16[2,256,256]{2,1,0:T(8,128)(2,1)}, u32[]{:S(2)}) copy-start(bf16[2,256,256]{2,1,0:T(8,128)(2,1)} %param.12) | copy-start | bytes 786436
  44.7 32.7 %copy-start.2 = (bf16[2,256,256]{2,1,0:T(8,128)(2,1)S(1)}, bf16[2,256,256]{2,1,0:T(8,128)(2,1)}, u32[]{:S(2)}) copy-start(bf16[2,256,256]{2,1,0:T(8,128)(2,1)} %param.13) | copy-start | bytes 786436
  44.7 32.9 %copy-start.4 = (bf16[256,256]{1,0:T(8,128)(2,1)S(1)}, bf16[256,256]{1,0:T(8,128)(2,1)}, u32[]{:S(2)}) copy-start(bf16[256,256]{1,0:T(8,128)(2,1)} %param.11) | copy-start | bytes 393220
  44.7 32.9 %copy-start.6 = (bf16[2,256,256]{2,1,0:T(8,128)(2,1)S(1)}, bf16[2,256,256]{2,1,0:T(8,128)(2,1)}, u32[]{:S(2)}) copy-start(bf16[2,256,256]{2,1,0:T(8,128)(2,1)} %param.14) | copy-start | bytes 786436
  44.7 10.6 %all-to-all-start = ((bf16[4,256,256]{2,1,0:T(8,128)(2,1)}), bf16[4,256,256]{2,1,0:T(8,128)(2,1)S(1)}, u32[]{:S(2)}, u32[]{:S(2)}) async-start(bf16[4,256,256]{2,1,0:T(8,128)(2,1)} %bitcast.12), calls=%async_computation | async-start | bytes 1048576 | tf_op jit(solution)/shard_map/all_to_all | solution.py:64
  48.4 83.0 %reduce-scatter.9.cloned.1.call-start = ((), (), s32[]{:S(2)}) async-start(), calls=%async_computation.13 | async-start | bytes 2359296 | tf_op jit(solution)/shard_map/reduce_scatter | solution.py:62
  95.7 60.3 %all-gather.8.cloned.1.call-start = ((), (), s32[]{:S(2)}) async-start(), calls=%async_computation.12 | async-start | bytes 1179648 | tf_op jit(solution)/shard_map/all_gather | solution.py:57
  133.1 31.0 %copy-start.5 = (bf16[256,256]{1,0:T(8,128)(2,1)S(1)}, bf16[256,256]{1,0:T(8,128)(2,1)}, u32[]{:S(2)}) copy-start(bf16[256,256]{1,0:T(8,128)(2,1)} %param.21) | copy-start | bytes 393220
  160.6 12.1 %all-to-all-start.1 = ((bf16[4,256,256]{2,1,0:T(8,128)(2,1)}), bf16[4,256,256]{2,1,0:T(8,128)(2,1)S(1)}, u32[]{:S(2)}, u32[]{:S(2)}) async-start(bf16[4,256,256]{2,1,0:T(8,128)(2,1)} %bitcast.17), calls=%async_computation.2 | async-start | bytes 1048576 | tf_op jit(solution)/shard_map/all_to_all | solution.py:64
  164.0 33.8 %all-gather.10.cloned.1.call-start = ((), (), s32[]{:S(2)}) async-start(), calls=%async_computation.14 | async-start | bytes 1179648 | tf_op jit(solution)/shard_map/all_gather | solution.py:57
  174.7 60.1 %reduce-scatter.11.cloned.1.call-start = ((), (), s32[]{:S(2)}) async-start(), calls=%async_computation.15 | async-start | bytes 2359296 | tf_op jit(solution)/shard_map/reduce_scatter | solution.py:62
  202.4 12.1 %all-to-all-start.2 = ((bf16[4,256,256]{2,1,0:T(8,128)(2,1)}), bf16[4,256,256]{2,1,0:T(8,128)(2,1)S(1)}, u32[]{:S(2)}, u32[]{:S(2)}) async-start(bf16[4,256,256]{2,1,0:T(8,128)(2,1)} %bitcast.22), calls=%async_computation.4 | async-start | bytes 1048576 | tf_op jit(solution)/shard_map/all_to_all | solution.py:64
  205.9 66.7 %reduce-scatter.15.cloned.1.call-start = ((), (), s32[]{:S(2)}) async-start(), calls=%async_computation.18 | async-start | bytes 2359296 | tf_op jit(solution)/shard_map/reduce_scatter | solution.py:112
  238.0 60.3 %reduce-scatter.17.cloned.1.call-start = ((), (), s32[]{:S(2)}) async-start(), calls=%async_computation.19 | async-start | bytes 327680 | tf_op jit(solution)/shard_map/reduce_scatter | solution.py:113
  272.6 51.8 %all-gather.12.cloned.1.call-start = ((), (), s32[]{:S(2)}) async-start(), calls=%async_computation.16 | async-start | bytes 1179648 | tf_op jit(solution)/shard_map/all_gather | solution.py:57
  273.5 87.9 %reduce-scatter.13.cloned.1.call-start = ((), (), s32[]{:S(2)}) async-start(), calls=%async_computation.17 | async-start | bytes 2359296 | tf_op jit(solution)/shard_map/reduce_scatter | solution.py:62
  291.3 128.0 %all-gather.14.cloned.1.call-start = ((), (), s32[]{:S(2)}) async-start(), calls=%async_computation.20 | async-start | bytes 2162688 | tf_op jit(solution)/shard_map/all_gather | solution.py:114
  329.0 12.2 %all-to-all-start.3 = ((bf16[4,256,256]{2,1,0:T(8,128)(2,1)}), bf16[4,256,256]{2,1,0:T(8,128)(2,1)S(1)}, u32[]{:S(2)}, u32[]{:S(2)}) async-start(bf16[4,256,256]{2,1,0:T(8,128)(2,1)} %bitcast.23), calls=%async_computation.6 | async-start | bytes 1048576 | tf_op jit(solution)/shard_map/all_to_all | solution.py:64
Sparse Core Ops, SparseCore 0:
  10.1 26.6 all-gather.5
  40.2 36.1 reduce-scatter.6
  95.8 35.5 reduce-scatter.8
  133.4 22.5 all-gather.7
  174.8 22.9 all-gather.9
  199.9 34.8 reduce-scatter.10
  238.1 34.3 reduce-scatter.14
  275.3 22.9 reduce-scatter.16
  300.5 23.8 all-gather.11
  326.6 34.8 reduce-scatter.12
  364.3 54.8 all-gather.13
